TPU v7x, 512 devices: a whole 4x8x8 slice. The times are simulated.
512 devices in a mesh: dp: 64 (over z, x, core), expert: 8 (over y).
Axes of the slice: x: 4, y: 8, z: 8, core: 2. Of those that a mesh axis runs over, the one named last changes fastest.
Arguments:
- tokens: bfloat16 [512, 4096], P('expert', 'dp'), may hold values from -6 to 6
- cotangent: bfloat16 [512, 4096], P('expert', 'dp'), may hold values from -6 to 6
- gate_logit: float32 [512], P('expert'), may hold values from -8 to 8
- routes: int32 [512, 2], P('expert'), may hold values from 0 to 7, all different within a row; in each aligned block of 64 rows (0 to 63, 64 to 127, ...) at most 32 rows name the same one
- w_up: bfloat16 [8, 14336, 4096], P('expert', 'dp'), may hold values from -0.09375 to 0.09375
- w_down: bfloat16 [8, 14336, 4096], P('expert', 'dp'), may hold values from -0.046875 to 0.046875
- basis: bfloat16 [4096, 256], P('dp'), may hold values from -0.09375 to 0.09375
- sketch: float32 [8, 256, 256], P('expert'), may hold values from -1 to 10, as said below
Outputs:
- token_grad: bfloat16 [512, 4096], P('expert', 'dp')
- sketch_next: float32 [8, 256, 256], P('expert')
- precond: float32 [8, 14336, 256], P('expert', 'dp')
Inputs may be any that keep to these rules, and one draw needn't show every extreme that they name: `routes`: each row names 2 different experts. Among the 64 tokens of one index of expert at most 32 name the same expert, and in some index that many do. `sketch`: each matrix is symmetric, and in every row its diagonal entry exceeds the sum of the magnitudes off the diagonal.
All inputs are finite; a program needn't handle non-finite values.
Results may differ from a plain program's by a relative error of at most 0.0064.
Values may be sent and summed in bfloat16 or wider, within the bound.
A program may use at most 128 MiB of HBM per device.

v0:
```python
import jax
import jax.numpy as jnp
from jax import lax
from jax.sharding import PartitionSpec as P

decay_rate = 0.9
damping = 1.0
highest = lax.Precision.HIGHEST


def per_device(tokens, cotangent, gate_logit, routes, w_up, w_down, basis, sketch):
    experts = lax.axis_size("expert")
    tok_rows = tokens.shape[0]
    width_local = tokens.shape[1]
    capacity = min(tok_rows, tok_rows * 4 // experts)
    slot_count = experts * capacity
    gate_first = jax.nn.sigmoid(gate_logit)
    gates = jnp.stack([gate_first, 1.0 - gate_first], axis=1)
    expert_ids = jnp.arange(experts, dtype=jnp.int32)
    chosen = routes[:, :, None] == expert_ids[None, None, :]
    hit_count = jnp.sum(chosen.astype(jnp.int32), axis=1)
    gate_by_expert = jnp.sum(chosen.astype(jnp.float32) * gates[:, :, None], axis=1)
    before = jnp.cumsum(hit_count, axis=0) - hit_count
    slot_of = expert_ids[None, :] * capacity + before
    slot_ids = jnp.arange(slot_count, dtype=jnp.int32)
    slot_match = (
        (slot_of[None, :, :] == slot_ids[:, None, None]) & (hit_count[None, :, :] > 0)
    ).astype(jnp.float32)
    table = jnp.sum(slot_match, axis=2)
    gate_slot = jnp.sum(slot_match * gate_by_expert[None, :, :], axis=(1, 2))
    table_b = table.astype(jnp.bfloat16)
    x_send = jnp.dot(table_b, tokens, preferred_element_type=jnp.float32).astype(jnp.bfloat16)
    cot_rows = jnp.dot(table_b, cotangent, preferred_element_type=jnp.float32)
    dy_send = (gate_slot[:, None] * cot_rows).astype(jnp.bfloat16)
    x_send = x_send.reshape(experts, capacity, width_local)
    dy_send = dy_send.reshape(experts, capacity, width_local)
    x_recv, dy_recv = (
        lax.all_to_all(x_send, "expert", split_axis=0, concat_axis=0, tiled=True),
        lax.all_to_all(dy_send, "expert", split_axis=0, concat_axis=0, tiled=True),
    )
    x_full, dy_full = (
        lax.all_gather(x_recv, "dp", axis=2, tiled=True),
        lax.all_gather(dy_recv, "dp", axis=2, tiled=True),
    )
    row_block = x_full.reshape(slot_count, -1)
    dy_block = dy_full.reshape(slot_count, -1)
    up_local = w_up[0]
    down_local = w_down[0]
    hidden = lax.dot_general(
        row_block, up_local, (((1,), (1,)), ((), ())), preferred_element_type=jnp.float32
    )
    back_grad = lax.dot_general(
        dy_block, down_local, (((1,), (1,)), ((), ())), preferred_element_type=jnp.float32
    )
    sigma_val = jax.nn.sigmoid(hidden)
    hidden_grad = (back_grad * sigma_val * (1.0 + hidden * (1.0 - sigma_val))).astype(jnp.bfloat16)
    partial_value = jnp.dot(hidden_grad, up_local, preferred_element_type=jnp.float32)
    summed = lax.psum_scatter(partial_value, "dp", scatter_dimension=1, tiled=True).astype(
        jnp.bfloat16
    )
    returned = lax.all_to_all(
        summed.reshape(experts, capacity, width_local),
        "expert",
        split_axis=0,
        concat_axis=0,
        tiled=True,
    )
    token_grad = lax.dot_general(
        table_b,
        returned.reshape(slot_count, width_local),
        (((0,), (0,)), ((), ())),
        preferred_element_type=jnp.float32,
    ).astype(jnp.bfloat16)
    basis_full = lax.all_gather(basis, "dp", axis=0, tiled=True)
    projected = jnp.dot(row_block, basis_full, preferred_element_type=jnp.float32).astype(
        jnp.bfloat16
    )
    coefficients = lax.dot_general(
        projected, hidden_grad, (((0,), (0,)), ((), ())), preferred_element_type=jnp.float32
    )
    gram_part = jnp.dot(coefficients, coefficients.T, precision=highest)
    total_hidden = w_up.shape[1] * lax.axis_size("dp")
    gram_total = lax.psum(gram_part, "dp") / total_hidden
    merged = decay_rate * sketch[0] + gram_total
    factor = jnp.linalg.cholesky(merged + damping * jnp.eye(merged.shape[0], dtype=jnp.float32))
    solved = damping * jax.scipy.linalg.cho_solve((factor, True), coefficients)
    return (token_grad, merged[None], solved.T[None])


def solution(mesh):
    in_specs = (
        P("expert", "dp"),
        P("expert", "dp"),
        P("expert"),
        P("expert", None),
        P("expert", "dp", None),
        P("expert", "dp", None),
        P("dp", None),
        P("expert", None, None),
    )
    out_specs = (P("expert", "dp"), P("expert", None, None), P("expert", "dp", None))
    return jax.shard_map(
        per_device, mesh=mesh, in_specs=in_specs, out_specs=out_specs, check_vma=False
    )
```

profile of v0, /device:TPU:1, one launch (start us, length us, event | category | flops | bytes accessed | tf_op | source)
XLA Modules:
  0.0 652.3 jit_solution(2081533431602891325)
XLA Ops:
  7.2 0.8 convert_reduce_fusion.1
  8.1 0.7 subtract_bitcast_fusion
  8.8 0.7 select_reduce_fusion.3
  9.8 0.3 convert_reduce_fusion
  10.1 0.9 fusion.16
  11.3 14.3 %all_to_all.15 = bf16[8,2,1024]{2,1,0:T(2,128)(2,1)S(1)} all-to-all(bf16[8,2,1024]{2,1,0:T(2,128)(2,1)S(1)} %reshape.113), channel_id=1, replica_groups=mesh['dp'=64,'expert'=8] {'expert'}, dimensions={0} | all-to-all | bytes 65536 | tf_op jit(solution)/shard_map/all_to_all | solution.py:39
  25.7 0.8 copy.44
  26.6 0.9 convolution_convert_fusion.1
  27.7 9.2 %all_to_all.16 = bf16[8,2,1024]{2,1,0:T(2,128)(2,1)S(1)} all-to-all(bf16[8,2,1024]{2,1,0:T(2,128)(2,1)S(1)} %reshape.115), channel_id=1, replica_groups=mesh['dp'=64,'expert'=8] {'expert'}, dimensions={0} | all-to-all | bytes 65536 | tf_op jit(solution)/shard_map/all_to_all | solution.py:38
  37.1 0.8 copy.47
  38.0 0.7 all-gather.8.cloned.1.call-update
  38.7 78.5 %all-gather.4.cloned.1.call-done = bf16[8,32,4096]{1,0,2:T(8,128)(2,1)} async-done(((bf16[8,32,64]{1,0,2:T(8,128)(2,1)}), bf16[8,32,4096]{1,0,2:T(8,128)(2,1)}) %all-gather.4.cloned.1.call-update) | async-done | bytes 2097168 | tf_op jit(solution)/shard_map/all_gather | solution.py:43
  117.2 9.3 %copy.45 = bf16[8,32,4096]{2,1,0:T(8,128)(2,1)} copy(bf16[8,32,4096]{1,0,2:T(8,128)(2,1)} %all-gather.4.cloned.1.call-done) | data formatting | bytes 4194304 | tf_op jit(solution)/shard_map/all_gather | solution.py:43
  126.5 80.1 %all-gather.6.cloned.1.call-done = bf16[8,32,4096]{1,0,2:T(8,128)(2,1)} async-done(((bf16[8,32,64]{1,0,2:T(8,128)(2,1)}), bf16[8,32,4096]{1,0,2:T(8,128)(2,1)}) %all-gather.6.cloned.1.call-update) | async-done | bytes 2097168 | tf_op jit(solution)/shard_map/all_gather | solution.py:42
  206.6 9.4 %copy.48 = bf16[8,32,4096]{2,1,0:T(8,128)(2,1)} copy(bf16[8,32,4096]{1,0,2:T(8,128)(2,1)} %all-gather.6.cloned.1.call-done) | data formatting | bytes 4194304 | tf_op jit(solution)/shard_map/all_gather | solution.py:42
  216.0 2.5 fusion.2
  218.7 0.8 fusion.12
  219.5 70.5 %all-gather.8.cloned.1.call-done = bf16[4096,256]{1,0:T(8,128)(2,1)} async-done(((bf16[64,256]{1,0:T(8,128)(2,1)}), bf16[4096,256]{1,0:T(8,128)(2,1)}) %all-gather.8.cloned.1.call-update) | async-done | bytes 2097168 | tf_op jit(solution)/shard_map/all_gather | solution.py:74
  290.0 3.1 fusion.15
  293.2 1.3 fusion.34
  294.8 2.9 fusion
  297.7 0.9 copy-done.2
  298.8 181.8 %all-reduce.3.cloned.1.call-done = f32[256,256]{0,1:T(8,128)} async-done(((f32[256,256]{0,1:T(8,128)}), f32[256,256]{0,1:T(8,128)}) %all-reduce.3.cloned.1.call-update) | async-done | bytes 262160 | tf_op jit(solution)/shard_map/psum | solution.py:83
  480.5 1.0 convert_add_fusion
  481.7 11.7 %cholesky.50 = f32[128,128]{1,0:T(8,128)S(1)} custom-call(f32[128,128]{1,0:T(8,128)S(1)} %cholesky.118), custom_call_target="Cholesky" | custom-call | tf_op jit(solution)/shard_map/jit(cholesky)/cholesky | solution.py:85
  493.5 9.8 %custom-call.18 = f32[1,128,128]{1,2,0:T(8,128)S(1)} custom-call(f32[1,128,128]{2,1,0:T(8,128)S(1)} %get-tuple-element.42), custom_call_target="InvertDiagBlocksLowerTriangular" | custom-call | tf_op jit(solution)/shard_map/jit(cholesky)/cholesky | solution.py:85
  503.5 0.3 convolution_subtract_fusion.2
  503.8 11.7 %cholesky.105 = f32[128,128]{1,0:T(8,128)S(1)} custom-call(f32[128,128]{1,0:T(8,128)S(1)} %convolution_subtract_fusion.2), custom_call_target="Cholesky" | custom-call | tf_op jit(solution)/shard_map/jit(cholesky)/cholesky | solution.py:85
  515.5 0.6 compare_reduce_fusion
  517.6 4.2 while.1
  517.8 0.6 fusion.57
  518.4 1.4 bitcast_dynamic-update-slice_fusion.2
  519.8 0.6 fusion.57
  520.4 1.4 bitcast_dynamic-update-slice_fusion.2
  521.8 19.7 %custom-call.19 = f32[2,128,128]{1,2,0:T(8,128)S(1)} custom-call(f32[2,128,128]{2,1,0:T(8,128)S(1)} %get-tuple-element.10), custom_call_target="InvertDiagBlocksLowerTriangular" | custom-call | tf_op jit(solution)/shard_map/jit(_cho_solve)/triangular_solve | solution.py:86
  541.5 0.2 fusion.19
  541.7 0.3 convolution_subtract_fusion.1
  542.0 0.3 fusion.27
  542.3 0.3 fusion.26
  542.8 0.3 fusion.25
  543.1 86.9 %reduce-scatter.2.cloned.1.call-done = f32[256,64]{0,1:T(8,128)} async-done(((f32[256,4096]{0,1:T(8,128)}), f32[256,64]{0,1:T(8,128)}) %reduce-scatter.2.cloned.1.call-update) | async-done | bytes 65552 | tf_op jit(solution)/shard_map/reduce_scatter | solution.py:58
  629.9 0.8 convert_element_type.37
  630.9 0.7 reshape.117
  631.6 6.5 all-to-all-start.2
  638.1 0.7 maximum_bitcast_fusion
  638.8 0.8 copy.53
  639.6 5.3 all-to-all-done.2
  645.0 0.7 convolution_convert_fusion.2
  (47 shorter events, 2.9 us)
Async XLA Ops:
  7.2 208.8 %copy-start = (bf16[1,224,4096]{2,1,0:T(8,128)(2,1)S(1)}, bf16[1,224,4096]{2,1,0:T(8,128)(2,1)}, u32[]{:S(2)}) copy-start(bf16[1,224,4096]{2,1,0:T(8,128)(2,1)} %param.12) | copy-start | bytes 5505028
  7.2 110.0 %all-gather.4.cloned.1.call-start = ((), (), s32[]{:S(2)}) async-start(), calls=%async_computation.4 | async-start | bytes 8519680 | tf_op jit(solution)/shard_map/all_gather | solution.py:43
  26.5 180.0 %all-gather.6.cloned.1.call-start = ((), (), s32[]{:S(2)}) async-start(), calls=%async_computation.5 | async-start | bytes 8519680 | tf_op jit(solution)/shard_map/all_gather | solution.py:42
  37.9 252.1 %all-gather.8.cloned.1.call-start = ((), (), s32[]{:S(2)}) async-start(), calls=%async_computation.7 | async-start | bytes 2129920 | tf_op jit(solution)/shard_map/all_gather | solution.py:74
  38.6 441.9 %all-reduce.3.cloned.1.call-start = ((), (), s32[]{:S(2)}) async-start(), calls=%async_computation.8 | async-start | bytes 524288 | tf_op jit(solution)/shard_map/psum | solution.py:83
  216.0 2.6 copy-start.1
  216.0 2.8 copy-start.3
  294.5 335.4 %reduce-scatter.2.cloned.1.call-start = ((), (), s32[]{:S(2)}) async-start(), calls=%async_computation.6 | async-start | bytes 4259840 | tf_op jit(solution)/shard_map/reduce_scatter | solution.py:58
  297.7 0.9 copy-start.2
  631.6 13.3 %all-to-all-start.2 = ((bf16[8,2,1024]{2,1,0:T(2,128)(2,1)}), bf16[8,2,1024]{2,1,0:T(2,128)(2,1)S(1)}, u32[]{:S(2)}, u32[]{:S(2)}) async-start(bf16[8,2,1024]{2,1,0:T(2,128)(2,1)} %reshape.117), calls=%async_computation.3 | async-start | bytes 65536 | tf_op jit(solution)/shard_map/all_to_all | solution.py:61
Sparse Core Ops, SparseCore 0:
  26.6 90.4 all-gather.3
  121.1 85.4 all-gather.5
  209.9 80.0 all-gather.7
  294.7 185.8 all-reduce.2
  485.1 144.7 reduce-scatter.1
where the time goes:
time: 658 us; the launch traced here: 652 us
  waiting for transfers between devices  504 us (77%)
  other arithmetic  58.9 us (9%)
  local copies, waits for them, and re-layouts  28.5 us (4%)
  blocking collectives  23.6 us (4%)
  matrix products  15.3 us (2%)
  between operations  15.3 us (2%)
  starting transfers between devices  6.84 us (1%)
    psum x1, waiting for transfers between devices, per_device(): gram_total = lax.psum(gram_part, 'dp') / total_hidden  182 us
    reduce_scatter x1, waiting for transfers between devices, per_device(): lax.psum_scatter(partial_value, 'dp', scatter_dimension=1, tiled=True)  86.9 us
    all_gather x1, waiting for transfers between devices, per_device(): lax.all_gather(x_recv, 'dp', axis=2, tiled=True)  80.1 us
    all_gather x1, waiting for transfers between devices, per_device(): lax.all_gather(dy_recv, 'dp', axis=2, tiled=True)  78.5 us
    all_gather x1, waiting for transfers between devices, per_device(): basis_full = lax.all_gather(basis, 'dp', axis=0, tiled=True)  70.5 us
    another operation x6, other arithmetic, per_device(): jnp.linalg.cholesky(merged + damping * jnp.eye(merged.shape[0], dtype=jnp...  34 us
    another operation x3, other arithmetic, per_device(): solved = damping * jax.scipy.linalg.cho_solve((factor, True), coefficients)  19.7 us
    all_to_all x1, blocking collectives, per_device(): lax.all_to_all(dy_send, 'expert', split_axis=0, concat_axis=0, tiled=True)  14.3 us
  transfers between devices with their start and end apart: 6, of which 6 were waited for; matrix products, arithmetic and copies ran while one was open for 14% of the time, Pallas kernels for 0%

commit v1 on v0

v1 whole, which is shorter than its diff:
```python
import functools

import jax
import jax.numpy as jnp
from jax import lax
from jax.experimental import pallas as pl
from jax.experimental.pallas import tpu as pltpu
from jax.sharding import PartitionSpec as P

decay_rate = 0.9
damping = 1.0
highest = lax.Precision.HIGHEST
MESH = pl.DeviceIdType.MESH
CORES = 2
WIDE = 4
bf16 = jnp.bfloat16
f32 = jnp.float32
VMEM = pl.BlockSpec(memory_space=pltpu.VMEM)
ANY = pl.BlockSpec(memory_space=pl.ANY)


def greet(axis, peers):
    barrier = pltpu.get_barrier_semaphore()
    for peer in peers:
        pl.semaphore_signal(barrier, inc=1, device_id={axis: peer}, device_id_type=MESH)
    pl.semaphore_wait(barrier, len(peers))


def remote(src, dst, send, recv, axis, peer):
    copy = pltpu.make_async_remote_copy(
        src_ref=src,
        dst_ref=dst,
        send_sem=send,
        recv_sem=recv,
        device_id={axis: peer},
        device_id_type=MESH,
    )
    copy.start()
    return copy


def exchange_kernel(n, src, dst, send, recv, own):
    me = lax.axis_index("expert")
    peers = [lax.rem(me + k, n) for k in range(1, n)]
    greet("expert", peers)
    copies = [
        remote(src.at[peer], dst.at[me], send.at[k], recv.at[k], "expert", peer)
        for k, peer in enumerate(peers)
    ]
    mine = pltpu.make_async_copy(src.at[me], dst.at[me], own)
    mine.start()
    for copy in copies:
        copy.wait()
    mine.wait()


def exchange(value, n, number):
    return pl.pallas_call(
        functools.partial(exchange_kernel, n),
        out_shape=jax.ShapeDtypeStruct(value.shape, value.dtype),
        in_specs=[VMEM],
        out_specs=VMEM,
        scratch_shapes=[
            pltpu.SemaphoreType.DMA((n,)),
            pltpu.SemaphoreType.DMA((n,)),
            pltpu.SemaphoreType.DMA,
        ],
        compiler_params=pltpu.CompilerParams(collective_id=number, has_side_effects=True),
    )(value)


def place(deep):
    me = lax.axis_index("dp")
    core = lax.rem(me, CORES)
    chip = me // CORES
    return chip // WIDE, lax.rem(chip, WIDE), core


def index_of(z, x, core):
    return (z * WIDE + x) * CORES + core


def gather_kernel(
    deep, x_in, dy_in, basis_in, up_hbm, down_hbm, r_out, c_out, gram_out,
    xs, dys, bases, up, down, hid, back, proj, sent, got, ring_send, ring_recv, share_send, share_recv,
):
    z, x, core = place(deep)
    other = 1 - core
    partner = index_of(z, x, other)
    sizes = {"z": deep, "x": WIDE}
    spot = {"z": z, "x": x}

    def near(axis, step):
        at = lax.rem(spot[axis] + step + sizes[axis], sizes[axis])
        return index_of(at, x, core) if axis == "z" else index_of(z, at, core)

    fetch_up = pltpu.make_async_copy(up_hbm, up, got.at[0])
    fetch_down = pltpu.make_async_copy(down_hbm, down, got.at[1])
    fetch_up.start()
    fetch_down.start()
    greet("dp", [near("z", 1), near("z", -1), near("x", 1), near("x", -1), partner])

    full = [xs, dys, bases]
    starts = [x_in, dy_in, basis_in]
    orders = [("z", "x"), ("x", "z"), ("z", "x")]
    own = []
    for t in range(3):
        copy = pltpu.make_async_copy(starts[t], full[t].at[z, x, core], sent.at[t])
        copy.start()
        own.append(copy)
    sends = []
    flows = []

    def block(t, axis, at, half=None):
        rows = slice(None) if half is None else pl.ds(half * 32, 32)
        return full[t].at[at, x, core, rows] if axis == "z" else full[t].at[z, at, core, rows]

    def slab(t, axis, at, half=None):
        if axis == "x":
            part = slice(None) if half is None else pl.ds(half * (deep // 2), deep // 2)
            return full[t].at[part, at, core]
        part = slice(None) if half is None else pl.ds(half * (WIDE // 2), WIDE // 2)
        return full[t].at[at, part, core]

    def ring_step(t, phase, axis, step, view):
        last = sizes[axis] // 2
        copies = []
        for way, sign in enumerate((1, -1)):
            at = lax.rem(spot[axis] - sign * (step - 1) + sizes[axis], sizes[axis])
            piece = view(t, axis, at, way if step == last else None)
            source = piece
            if phase == 0 and step == 1:
                source = starts[t] if step != last else starts[t].at[pl.ds(way * 32, 32)]
            copies.append(
                remote(
                    source, piece, ring_send.at[t, phase, way, step - 1],
                    ring_recv.at[t, phase, way, step - 1], "dp", near(axis, sign),
                )
            )
        sends.extend(copies)
        return copies

    shares = []

    def share(t, axis, at):
        piece = slab(t, axis, at)
        number = 0
        for old in shares:
            number += old[0] == t
        copy = remote(
            piece, piece, share_send.at[t, number], share_recv.at[t, number], "dp", partner
        )
        shares.append((t, copy))

    def stages(t):
        first, second = orders[t]
        for step in range(1, sizes[first] // 2 + 1):
            copies = ring_step(t, 0, first, step, block)
            yield
            for copy in copies:
                copy.wait_recv()
        own[t].wait()
        at = spot[second]
        n = sizes[second]
        copies = ring_step(t, 1, second, 1, slab)
        share(t, second, at)
        yield
        for step in range(1, n // 2):
            for copy in copies:
                copy.wait_recv()
            copies = ring_step(t, 1, second, step + 1, slab)
            share(t, second, lax.rem(at - step + n, n))
            share(t, second, lax.rem(at + step, n))
            yield
        for copy in copies:
            copy.wait_recv()
        share(t, second, lax.rem(at + n // 2, n))

    flows = [stages(t) for t in range(3)]
    while flows:
        for flow in list(flows):
            if next(flow, flow) is flow:
                flows.remove(flow)
    fetch_up.wait()
    fetch_down.wait()
    for copy in sends:
        copy.wait_send()
    for _, copy in shares:
        copy.wait()

    chunk = WIDE * CORES * 64
    hid[...] = jnp.zeros_like(hid)
    back[...] = jnp.zeros_like(back)
    proj[...] = jnp.zeros_like(proj)
    turned = (((0,), (0,)), ((), ()))

    def forward(at, carry):
        columns = pl.ds(pl.multiple_of(at * chunk, chunk), chunk)
        x_part = xs[at].reshape(chunk, 256)
        dy_part = dys[at].reshape(chunk, 256)
        basis_part = bases[at].reshape(chunk, 256)
        hid[...] += jnp.dot(up[:, columns], x_part, preferred_element_type=f32)
        back[...] += jnp.dot(down[:, columns], dy_part, preferred_element_type=f32)
        proj[...] += lax.dot_general(x_part, basis_part, turned, preferred_element_type=f32)
        return carry

    lax.fori_loop(0, deep, forward, 0)
    hidden = hid[...]
    sigma = jax.nn.sigmoid(hidden)
    grad = (back[...] * sigma * (1.0 + hidden * (1.0 - sigma))).astype(bf16)
    coef = jnp.dot(grad, proj[...].astype(bf16), preferred_element_type=f32)
    c_out[...] = coef
    gram_out[...] = lax.dot_general(
        coef, coef, turned, precision=highest, preferred_element_type=f32
    )

    def rows(at, carry):
        columns = pl.ds(pl.multiple_of(at * chunk, chunk), chunk)
        part = lax.dot_general(up[:, columns], grad, turned, preferred_element_type=f32)
        r_out[at] = part.astype(bf16).reshape(WIDE, CORES, 64, 256)
        return carry

    lax.fori_loop(0, deep, rows, 0)


def gather_compute(x_t, dy_t, basis, up, down, deep):
    units, width = up.shape
    blocks = (deep, WIDE, CORES, 64, 256)
    steps = max(deep, WIDE)
    return pl.pallas_call(
        functools.partial(gather_kernel, deep),
        out_shape=(
            jax.ShapeDtypeStruct(blocks, bf16),
            jax.ShapeDtypeStruct((units, 256), f32),
            jax.ShapeDtypeStruct((256, 256), f32),
        ),
        in_specs=[VMEM, VMEM, VMEM, ANY, ANY],
        out_specs=(VMEM, VMEM, VMEM),
        scratch_shapes=[
            pltpu.VMEM(blocks, bf16),
            pltpu.VMEM(blocks, bf16),
            pltpu.VMEM(blocks, bf16),
            pltpu.VMEM((units, width), bf16),
            pltpu.VMEM((units, width), bf16),
            pltpu.VMEM((units, 256), f32),
            pltpu.VMEM((units, 256), f32),
            pltpu.VMEM((256, 256), f32),
            pltpu.SemaphoreType.DMA((3,)),
            pltpu.SemaphoreType.DMA((2,)),
            pltpu.SemaphoreType.DMA((3, 2, 2, steps // 2)),
            pltpu.SemaphoreType.DMA((3, 2, 2, steps // 2)),
            pltpu.SemaphoreType.DMA((3, steps)),
            pltpu.SemaphoreType.DMA((3, steps)),
        ],
        compiler_params=pltpu.CompilerParams(
            collective_id=1, has_side_effects=True, vmem_limit_bytes=40 << 20
        ),
    )(x_t, dy_t, basis, up, down)


def reduce_kernel(
    deep, r_in, gram_in, r_out, gram_out,
    g0, gsum, gx, gz, r0, rsum, rx, r1, rz, core_send, core_recv, x_send, x_recv, z_send, z_recv,
):
    z, x, core = place(deep)
    other = 1 - core
    partner = index_of(z, x, other)
    x_at = [lax.rem(x + k, WIDE) for k in range(1, WIDE)]
    z_at = [lax.rem(z + k, deep) for k in range(1, deep)]
    x_peers = [index_of(z, at, core) for at in x_at]
    z_peers = [index_of(at, x, core) for at in z_at]
    greet("dp", [partner] + x_peers + z_peers)

    def to_core(number, src, dst):
        return remote(src, dst, core_send.at[number], core_recv.at[number], "dp", partner)

    def along_x(number, pairs):
        return [
            remote(src, dst, x_send.at[number, k], x_recv.at[number, k], "dp", x_peers[k])
            for k, (src, dst) in enumerate(pairs)
        ]

    def along_z(number, pairs):
        return [
            remote(src, dst, z_send.at[number, k], z_recv.at[number, k], "dp", z_peers[k])
            for k, (src, dst) in enumerate(pairs)
        ]

    gram_core = to_core(0, gram_in.at[other], g0)
    r_core = to_core(1, r_in.at[:, :, other], r0)

    gram_core.wait_recv()
    gsum[...] = gram_in[core] + g0[...]
    gram_x = along_x(0, [(gsum.at[at], gx.at[x]) for at in x_at])

    r_core.wait_recv()

    def add_core(at, carry):
        rsum[at] = (r_in[at, :, core].astype(f32) + r0[at].astype(f32)).astype(bf16)
        return carry

    lax.fori_loop(0, deep, add_core, 0)

    for copy in gram_x:
        copy.wait_recv()
    total = gsum[x]
    for at in x_at:
        total = total + gx[at]
    gz[z] = total
    gram_z = along_z(0, [(gz.at[z], gz.at[z]) for _ in z_at])
    r_x = along_x(1, [(rsum.at[:, at], rx.at[x]) for at in x_at])

    for copy in gram_z:
        copy.wait_recv()
    total = gz[0]
    for at in range(1, deep):
        total = total + gz[at]
    gram_out[core, x] = total
    gram_back = along_x(2, [(gram_out.at[core, x], gram_out.at[core, x]) for _ in x_at])

    for copy in r_x:
        copy.wait_recv()

    def add_x(at, carry):
        part = rsum[at, x].astype(f32)
        for peer in x_at:
            part = part + rx[peer, at].astype(f32)
        r1[at] = part.astype(bf16)
        return carry

    lax.fori_loop(0, deep, add_x, 0)
    r_z = along_z(1, [(r1.at[at], rz.at[z]) for at in z_at])
    for copy in gram_back:
        copy.wait_recv()
    gram_last = to_core(2, gram_out.at[core], gram_out.at[core])
    for copy in r_z:
        copy.wait_recv()
    part = r1[z].astype(f32)
    for at in z_at:
        part = part + rz[at].astype(f32)
    r_out[...] = part.astype(bf16)
    gram_last.wait_recv()
    for copy in [gram_core, r_core, gram_last] + gram_x + r_x + gram_back + gram_z + r_z:
        copy.wait_send()


def reduce_all(r_part, gram_part, deep):
    rows = 256 // (CORES * WIDE)
    gram_shape = (CORES, WIDE, rows, 256)
    r_sum, gram_sum = pl.pallas_call(
        functools.partial(reduce_kernel, deep),
        out_shape=(
            jax.ShapeDtypeStruct((64, 256), bf16),
            jax.ShapeDtypeStruct(gram_shape, f32),
        ),
        in_specs=[VMEM, VMEM],
        out_specs=(VMEM, VMEM),
        scratch_shapes=[
            pltpu.VMEM((WIDE, rows, 256), f32),
            pltpu.VMEM((WIDE, rows, 256), f32),
            pltpu.VMEM((WIDE, rows, 256), f32),
            pltpu.VMEM((deep, rows, 256), f32),
            pltpu.VMEM((deep, WIDE, 64, 256), bf16),
            pltpu.VMEM((deep, WIDE, 64, 256), bf16),
            pltpu.VMEM((WIDE, deep, 64, 256), bf16),
            pltpu.VMEM((deep, 64, 256), bf16),
            pltpu.VMEM((deep, 64, 256), bf16),
            pltpu.SemaphoreType.DMA((3,)),
            pltpu.SemaphoreType.DMA((3,)),
            pltpu.SemaphoreType.DMA((3, WIDE)),
            pltpu.SemaphoreType.DMA((3, WIDE)),
            pltpu.SemaphoreType.DMA((2, deep)),
            pltpu.SemaphoreType.DMA((2, deep)),
        ],
        compiler_params=pltpu.CompilerParams(
            collective_id=2, has_side_effects=True, vmem_limit_bytes=40 << 20
        ),
    )(r_part, gram_part.reshape(gram_shape))
    return r_sum, gram_sum.reshape(256, 256)


def per_device(tokens, cotangent, gate_logit, routes, w_up, w_down, basis, sketch):
    experts = lax.axis_size("expert")
    deep = lax.axis_size("dp") // (WIDE * CORES)
    tok_rows, width_local = tokens.shape
    capacity = min(tok_rows, tok_rows * 4 // experts)
    slot_count = experts * capacity
    gate_first = jax.nn.sigmoid(gate_logit)
    gates = jnp.stack([gate_first, 1.0 - gate_first], axis=1)
    expert_ids = jnp.arange(experts, dtype=jnp.int32)
    chosen = routes[:, :, None] == expert_ids[None, None, :]
    hit_count = jnp.sum(chosen.astype(jnp.int32), axis=1)
    gate_by_expert = jnp.sum(chosen.astype(f32) * gates[:, :, None], axis=1)
    before = jnp.cumsum(hit_count, axis=0) - hit_count
    slot_of = expert_ids[None, :] * capacity + before
    slot_ids = jnp.arange(slot_count, dtype=jnp.int32)
    slot_match = (
        (slot_of[None, :, :] == slot_ids[:, None, None]) & (hit_count[None, :, :] > 0)
    ).astype(f32)
    table = jnp.sum(slot_match, axis=2)
    gate_slot = jnp.sum(slot_match * gate_by_expert[None, :, :], axis=(1, 2))
    table_b = table.astype(bf16)
    both = jnp.concatenate([tokens, cotangent], axis=1)
    picked = jnp.dot(table_b, both, preferred_element_type=f32)
    scale = jnp.where(jnp.arange(2 * width_local)[None, :] < width_local, 1.0, gate_slot[:, None])
    packed = (picked * scale).astype(bf16).reshape(experts, capacity, 2 * width_local)
    arrived = exchange(packed, experts, 0).reshape(slot_count, 2 * width_local).T
    r_part, coef_t, gram_part = gather_compute(
        arrived[:width_local], arrived[width_local:], basis, w_up[0], w_down[0], deep
    )
    r_sum, gram_total = reduce_all(r_part, gram_part, deep)
    rows = jnp.pad(r_sum.T, ((0, 0), (0, 128 - width_local)))
    returned = exchange(rows.reshape(experts, capacity, 128), experts, 3)
    token_grad = lax.dot_general(
        table_b,
        returned.reshape(slot_count, 128)[:, :width_local],
        (((0,), (0,)), ((), ())),
        preferred_element_type=f32,
    ).astype(bf16)
    total_hidden = w_up.shape[1] * lax.axis_size("dp")
    merged = decay_rate * sketch[0] + gram_total / total_hidden
    factor = jnp.linalg.cholesky(merged + damping * jnp.eye(merged.shape[0], dtype=f32))
    solved = damping * jax.scipy.linalg.cho_solve((factor, True), coef_t.T)
    return (token_grad, merged[None], solved.T[None])


def solution(mesh):
    in_specs = (
        P("expert", "dp"),
        P("expert", "dp"),
        P("expert"),
        P("expert", None),
        P("expert", "dp", None),
        P("expert", "dp", None),
        P("dp", None),
        P("expert", None, None),
    )
    out_specs = (P("expert", "dp"), P("expert", None, None), P("expert", "dp", None))
    return jax.shard_map(
        per_device, mesh=mesh, in_specs=in_specs, out_specs=out_specs, check_vma=False
    )
```

time: 658 us -> 181 us (0.28)
  waiting for transfers between devices: 504 us -> 0 us
  Pallas kernels: 0 us -> 102 us
  blocking collectives: 23.6 us -> 0 us
  local copies, waits for them, and re-layouts: 28.5 us -> 11.1 us
  between operations: 15.3 us -> 2.2 us
  matrix products: 15.3 us -> 5.18 us
  starting transfers between devices: 6.84 us -> 0 us
    all_gather x3 -> x0, waiting for transfers between devices: 229 us -> none  [the longest x1 80.1 us: per_device(): lax.all_gather(x_recv, 'dp', axis=2, tiled=True)]
    psum x1 -> x0, waiting for transfers between devices: 182 us -> none  [per_device(): gram_total = lax.psum(gram_part, 'dp') / total_hidden]
    pallas_call x0 -> x4, Pallas kernels: none -> 102 us  [the longest x1 53.7 us: gather_compute(): pl.pallas_call(functools.partial(gather_kernel, deep), out_shape=(jax.Sha...]
    reduce_scatter x1 -> x0, waiting for transfers between devices: 86.9 us -> none  [per_device(): lax.psum_scatter(partial_value, 'dp', scatter_dimension=1, tiled=True)]
    all_to_all x2 -> x0, blocking collectives: 23.6 us -> none  [the longest x1 14.3 us: per_device(): lax.all_to_all(dy_send, 'expert', split_axis=0, concat_axis=0, tiled=True)]
    all_gather x2 -> x0, local copies, waits for them, and re-layouts: 18.7 us -> none  [the longest x1 9.39 us: per_device(): lax.all_gather(x_recv, 'dp', axis=2, tiled=True)]
    dot_general x8 -> x2, matrix products: 13.3 us -> 3.17 us  [the longest x1 1.59 us: per_device(): picked = jnp.dot(table_b, both, preferred_element_type=f32)]
  transfers between devices with their start and end apart: 6 -> 0, of which waited for: 6 -> 0; matrix products, arithmetic and copies ran while one was open for 14% -> 0% of each run, Pallas kernels for 0% -> 0%
where the time goes in v1:
time: 181 us; the launch traced here: 178 us
  Pallas kernels  102 us (56%)
  other arithmetic  57.2 us (32%)
  local copies, waits for them, and re-layouts  11.1 us (6%)
  matrix products  5.18 us (3%)
  between operations  2.2 us (1%)
    pallas_call x1, Pallas kernels, gather_compute(): pl.pallas_call(functools.partial(gather_kernel, deep), out_shape=(jax.Sha...  53.7 us
    another operation x6, other arithmetic, per_device(): jnp.linalg.cholesky(merged + damping * jnp.eye(merged.shape[0], dtype=f32))  33.9 us
    pallas_call x1, Pallas kernels, reduce_all(): pl.pallas_call(functools.partial(reduce_kernel, deep), out_shape=(jax.Sha...  28.5 us
    pallas_call x2, Pallas kernels, exchange(): pl.pallas_call(functools.partial(exchange_kernel, n), out_shape=jax.Shape...  20.1 us
    another operation x3, other arithmetic, per_device(): solved = damping * jax.scipy.linalg.cho_solve((factor, True), coef_t.T)  19.9 us
    unnamed x11, local copies, waits for them, and re-layouts  4.84 us
    another operation x6, local copies, waits for them, and re-layouts  3.95 us

profile of v1, /device:TPU:1, one launch (start us, length us, event | category | flops | bytes accessed | tf_op | source)
XLA Modules:
  0.0 178.0 jit_solution(17018510813006994182)
XLA Ops:
  0.6 0.7 convert_reduce_fusion.1
  1.3 0.1 copy.29
  1.4 0.1 reduce_window_sum.11
  1.5 0.7 subtract_bitcast_fusion
  2.2 0.7 select_reduce_fusion.3
  2.9 0.1 copy.32
  3.0 0.1 copy.31
  3.1 0.3 convert_reduce_fusion
  3.4 1.6 fusion
  5.0 10.7 %shard_map.103 = bf16[8,32,128]{2,1,0:T(8,128)(2,1)} custom-call(bf16[8,32,128]{2,1,0:T(8,128)(2,1)} %bitcast.73), custom_call_target="tpu_custom_call" | custom-call | tf_op jit(solution)/shard_map/pallas_call | solution.py:58
  15.7 0.9 copy.33
  16.7 0.0 copy-start
  16.7 1.5 copy-done
  18.2 1.5 copy-done.1
  19.7 0.8 copy-done.2
  20.5 53.7 %shard_map.104 = (bf16[8,4,2,64,256]{4,3,2,1,0:T(8,128)(2,1)S(1)}, f32[224,256]{1,0:T(8,128)S(1)}, f32[256,256]{1,0:T(8,128)S(1)}) custom-call(bf16[64,256]{1,0:T(8,128)(2,1)S(1)} %get-tuple-element.49.x_in, bf16[64,256]{1,0:T(8,128)(2,1)S(1)} %get-tuple-element.48.dy_in, bf16[64,256]{1,0:T(8,128)(2,1)S(1)} %copy-done.2, bf16[224,4096]{1,0:T(8,128)(2,1)S(1)} %bitcast.61, ...), custom_call_target="tpu_custom_call" | custom-call | tf_op jit(solution)/shard_map/pallas_call | solution.py:230
  74.1 0.0 copy-start.3
  74.1 28.5 %shard_map.105 = (bf16[64,256]{1,0:T(8,128)(2,1)S(1)}, f32[2,4,32,256]{3,2,1,0:T(8,128)S(1)}) custom-call(bf16[8,4,2,64,256]{4,3,2,1,0:T(8,128)(2,1)S(1)} %get-tuple-element.8.r_in, f32[2,4,32,256]{3,2,1,0:T(8,128)S(1)} %bitcast.63), custom_call_target="tpu_custom_call" | custom-call | tf_op jit(solution)/shard_map/pallas_call | solution.py:350
  102.7 0.1 copy.37
  102.8 0.0 copy-done.3
  102.8 0.1 copy.35
  103.0 0.1 copy.38
  103.2 11.7 %cholesky.50 = f32[128,128]{1,0:T(8,128)S(1)} custom-call(f32[128,128]{1,0:T(8,128)S(1)} %cholesky.118), custom_call_target="Cholesky" | custom-call | tf_op jit(solution)/shard_map/jit(cholesky)/cholesky | solution.py:422
  115.0 9.8 %custom-call.18 = f32[1,128,128]{1,2,0:T(8,128)S(1)} custom-call(f32[1,128,128]{2,1,0:T(8,128)S(1)} %get-tuple-element.47), custom_call_target="InvertDiagBlocksLowerTriangular" | custom-call | tf_op jit(solution)/shard_map/jit(cholesky)/cholesky | solution.py:422
  124.8 0.2 constant_dynamic-update-slice_fusion.1
  125.0 0.3 convolution_subtract_fusion.2
  125.3 11.7 %cholesky.105 = f32[128,128]{1,0:T(8,128)S(1)} custom-call(f32[128,128]{1,0:T(8,128)S(1)} %convolution_subtract_fusion.2), custom_call_target="Cholesky" | custom-call | tf_op jit(solution)/shard_map/jit(cholesky)/cholesky | solution.py:422
  137.0 0.6 compare_reduce_fusion
  139.0 0.1 triangular_solve.69
  139.1 4.0 %while.1 = (s32[]{:T(128)}, f32[256,256]{1,0:T(8,128)S(1)}, s32[2,2]{1,0:T(2,128)S(1)}, f32[2,128,128]{2,1,0:T(8,128)S(1)}, s32[]{:T(128)}) while((s32[]{:T(128)}, f32[256,256]{1,0:T(8,128)S(1)}, s32[2,2]{1,0:T(2,128)S(1)}, f32[2,128,128]{2,1,0:T(8,128)S(1)}, s32[]{:T(128)}) %tuple.33), condition=%wide.while_cond, body=%wide.while_body.sunk | while | flops 2 | bytes 131181 | solution.py:423
  139.1 0.6 fusion.33
  139.7 1.4 bitcast_dynamic-update-slice_fusion.2
  141.1 0.6 fusion.33
  141.7 1.4 bitcast_dynamic-update-slice_fusion.2
  143.1 19.9 %custom-call.19 = f32[2,128,128]{1,2,0:T(8,128)S(1)} custom-call(f32[2,128,128]{2,1,0:T(8,128)S(1)} %get-tuple-element.20), custom_call_target="InvertDiagBlocksLowerTriangular" | custom-call | tf_op jit(solution)/shard_map/jit(_cho_solve)/triangular_solve | solution.py:423
  163.0 0.2 fusion.4
  163.3 0.3 convolution_subtract_fusion.1
  163.5 0.2 fusion.12
  163.8 0.3 fusion.11
  164.1 0.2 convolution_subtract_fusion
  164.3 0.3 fusion.10
  164.6 0.7 maximum_bitcast_fusion
  165.3 0.1 copy.40
  165.4 0.7 pad.5.clone
  166.1 9.4 %shard_map.106 = bf16[8,32,128]{2,1,0:T(8,128)(2,1)} custom-call(bf16[8,32,128]{2,1,0:T(8,128)(2,1)} %bitcast.71), custom_call_target="tpu_custom_call" | custom-call | tf_op jit(solution)/shard_map/pallas_call | solution.py:58
  175.4 1.6 convolution_convert_fusion
  177.0 0.1 copy.36
  177.2 0.8 copy.39
  (21 shorter events, 0.3 us)
Async XLA Ops:
  16.7 1.5 copy-start
  18.2 1.5 copy-start.1
  19.7 0.8 copy-start.2
  74.1 28.7 %copy-start.3 = (f32[1,256,256]{2,1,0:T(8,128)S(1)}, f32[1,256,256]{2,1,0:T(8,128)}, u32[]{:S(2)}) copy-start(f32[1,256,256]{2,1,0:T(8,128)} %param.15) | copy-start | bytes 786436

commit v2 on v1

--- a/solution.py
+++ b/solution.py
@@ -253,23 +253,70 @@
             pltpu.SemaphoreType.DMA((3, steps)),
         ],
         compiler_params=pltpu.CompilerParams(
-            collective_id=1, has_side_effects=True, vmem_limit_bytes=40 << 20
+            collective_id=1, has_side_effects=True, vmem_limit_bytes=60 << 20
         ),
     )(x_t, dy_t, basis, up, down)
 
 
+def invert(matrix):
+    n, group = 128, 16
+    lane = lax.broadcasted_iota(jnp.int32, (1, n), 1)
+    row = lax.broadcasted_iota(jnp.int32, (group, n), 0)
+
+    def pivots(_, parts):
+        top, rest = parts
+        for k in range(0, group, 2):
+            first = jnp.broadcast_to(top[:, k : k + 1], (group, n))
+            second = jnp.broadcast_to(top[:, k + 1 : k + 2], (group, n))
+            first_rest = jnp.broadcast_to(rest[:, k : k + 1], (n - group, n))
+            second_rest = jnp.broadcast_to(rest[:, k + 1 : k + 2], (n - group, n))
+            a, b, d = first[k : k + 1], first[k + 1 : k + 2], second[k + 1 : k + 2]
+            a_inv = 1.0 / a
+            slope = b * a_inv
+            d_inv = 1.0 / (d - b * slope)
+            p12 = -slope * d_inv
+            p11 = a_inv - slope * p12
+            at_first, at_second = lane == k, lane == k + 1
+            row_a, row_b = top[k : k + 1], top[k + 1 : k + 2]
+            u_a = p11 * row_a + p12 * row_b
+            u_b = p12 * row_a + d_inv * row_b
+            u_a = jnp.where(at_first, p11, jnp.where(at_second, p12, u_a))
+            u_b = jnp.where(at_first, p12, jnp.where(at_second, d_inv, u_b))
+            inside = at_first | at_second
+            rest = jnp.where(inside, 0.0, rest) - first_rest * u_a - second_rest * u_b
+            top = jnp.where(inside, 0.0, top) - first * u_a - second * u_b
+            top = jnp.where(row == k, u_a, jnp.where(row == k + 1, u_b, top))
+        turned = pltpu.roll(jnp.concatenate([rest, top], axis=0), n - group, 1)
+        return turned[:group], turned[group:]
+
+    top, rest = lax.fori_loop(0, n // group, pivots, (matrix[:group], matrix[group:]))
+    return jnp.concatenate([top, rest], axis=0)
+
+
+def exact(left, right, dims=(((1,), (0,)), ((), ()))):
+    return lax.dot_general(left, right, dims, precision=highest, preferred_element_type=f32)
+
+
 def reduce_kernel(
-    deep, r_in, gram_in, r_out, gram_out,
-    g0, gsum, gx, gz, r0, rsum, rx, r1, rz, core_send, core_recv, x_send, x_recv, z_send, z_recv,
+    deep, experts, hidden_total, r_in, gram_in, sketch_in, coef_in, back_out, merged_out, solved_out,
+    g0, gsum, gx, gz, gram_out, r0, rsum, rx, r1, rz, ready,
+    core_send, core_recv, x_send, x_recv, z_send, z_recv, y_send, y_recv, y_own,
 ):
     z, x, core = place(deep)
+    me_y = lax.axis_index("expert")
     other = 1 - core
     partner = index_of(z, x, other)
     x_at = [lax.rem(x + k, WIDE) for k in range(1, WIDE)]
     z_at = [lax.rem(z + k, deep) for k in range(1, deep)]
+    y_at = [lax.rem(me_y + k, experts) for k in range(1, experts)]
     x_peers = [index_of(z, at, core) for at in x_at]
     z_peers = [index_of(at, x, core) for at in z_at]
-    greet("dp", [partner] + x_peers + z_peers)
+    barrier = pltpu.get_barrier_semaphore()
+    for peer in y_at:
+        pl.semaphore_signal(barrier, inc=1, device_id={"expert": peer}, device_id_type=MESH)
+    for peer in [partner] + x_peers + z_peers:
+        pl.semaphore_signal(barrier, inc=1, device_id={"dp": peer}, device_id_type=MESH)
+    pl.semaphore_wait(barrier, 1 + len(x_peers) + len(z_peers) + len(y_at))
 
     def to_core(number, src, dst):
         return remote(src, dst, core_send.at[number], core_recv.at[number], "dp", partner)
@@ -317,6 +364,22 @@
         total = total + gz[at]
     gram_out[core, x] = total
     gram_back = along_x(2, [(gram_out.at[core, x], gram_out.at[core, x]) for _ in x_at])
+    for copy in gram_back:
+        copy.wait_recv()
+    gram_last = to_core(2, gram_out.at[core], gram_out.at[core])
+    gram_last.wait_recv()
+
+    merged = decay_rate * sketch_in[...] + gram_out[...].reshape(256, 256) / hidden_total
+    merged_out[...] = merged
+    half = 128
+    eye = (
+        lax.broadcasted_iota(jnp.int32, (half, half), 0)
+        == lax.broadcasted_iota(jnp.int32, (half, half), 1)
+    ).astype(f32) * damping
+    corner = merged[:half, half:]
+    upper = invert(merged[:half, :half] + eye)
+    ratio = exact(upper, corner)
+    lower = merged[half:, half:] + eye - exact(merged[half:, :half], ratio)
 
     for copy in r_x:
         copy.wait_recv()
@@ -330,53 +393,75 @@
 
     lax.fori_loop(0, deep, add_x, 0)
     r_z = along_z(1, [(r1.at[at], rz.at[z]) for at in z_at])
-    for copy in gram_back:
-        copy.wait_recv()
-    gram_last = to_core(2, gram_out.at[core], gram_out.at[core])
+
+    left, right = coef_in[:, :half], coef_in[:, half:]
+    right = right - exact(left, ratio)
+    left = exact(left, upper)
     for copy in r_z:
         copy.wait_recv()
     part = r1[z].astype(f32)
     for at in z_at:
         part = part + rz[at].astype(f32)
-    r_out[...] = part.astype(bf16)
-    gram_last.wait_recv()
-    for copy in [gram_core, r_core, gram_last] + gram_x + r_x + gram_back + gram_z + r_z:
+    part = jnp.concatenate([part, jnp.zeros_like(part)], axis=0)
+    ready[...] = part.T.astype(bf16).reshape(ready.shape)
+    r_y = [
+        remote(ready.at[at], back_out.at[me_y], y_send.at[k], y_recv.at[k], "expert", at)
+        for k, at in enumerate(y_at)
+    ]
+    mine = pltpu.make_async_copy(ready.at[me_y], back_out.at[me_y], y_own)
+    mine.start()
+
+    right = exact(right, invert(lower))
+    solved_out[:, half:] = right * damping
+    left = left - exact(right, ratio, (((1,), (1,)), ((), ())))
+    solved_out[:, :half] = left * damping
+
+    for copy in r_y:
+        copy.wait_recv()
+    mine.wait()
+    for copy in [gram_core, r_core, gram_last] + gram_x + r_x + gram_back + gram_z + r_z + r_y:
         copy.wait_send()
 
 
-def reduce_all(r_part, gram_part, deep):
+def reduce_all(r_part, gram_part, sketch, coef_t, deep, experts, hidden_total):
     rows = 256 // (CORES * WIDE)
     gram_shape = (CORES, WIDE, rows, 256)
-    r_sum, gram_sum = pl.pallas_call(
-        functools.partial(reduce_kernel, deep),
+    send_shape = (experts, 256 // experts, 128)
+    return pl.pallas_call(
+        functools.partial(reduce_kernel, deep, experts, hidden_total),
         out_shape=(
-            jax.ShapeDtypeStruct((64, 256), bf16),
-            jax.ShapeDtypeStruct(gram_shape, f32),
+            jax.ShapeDtypeStruct(send_shape, bf16),
+            jax.ShapeDtypeStruct((256, 256), f32),
+            jax.ShapeDtypeStruct(coef_t.shape, f32),
         ),
-        in_specs=[VMEM, VMEM],
-        out_specs=(VMEM, VMEM),
+        in_specs=[VMEM] * 4,
+        out_specs=(VMEM,) * 3,
         scratch_shapes=[
             pltpu.VMEM((WIDE, rows, 256), f32),
             pltpu.VMEM((WIDE, rows, 256), f32),
             pltpu.VMEM((WIDE, rows, 256), f32),
             pltpu.VMEM((deep, rows, 256), f32),
+            pltpu.VMEM(gram_shape, f32),
             pltpu.VMEM((deep, WIDE, 64, 256), bf16),
             pltpu.VMEM((deep, WIDE, 64, 256), bf16),
             pltpu.VMEM((WIDE, deep, 64, 256), bf16),
             pltpu.VMEM((deep, 64, 256), bf16),
             pltpu.VMEM((deep, 64, 256), bf16),
+            pltpu.VMEM(send_shape, bf16),
             pltpu.SemaphoreType.DMA((3,)),
             pltpu.SemaphoreType.DMA((3,)),
             pltpu.SemaphoreType.DMA((3, WIDE)),
             pltpu.SemaphoreType.DMA((3, WIDE)),
             pltpu.SemaphoreType.DMA((2, deep)),
             pltpu.SemaphoreType.DMA((2, deep)),
+            pltpu.SemaphoreType.DMA((experts,)),
+            pltpu.SemaphoreType.DMA((experts,)),
+            pltpu.SemaphoreType.DMA,
         ],
         compiler_params=pltpu.CompilerParams(
             collective_id=2, has_side_effects=True, vmem_limit_bytes=40 << 20
         ),
-    )(r_part, gram_part.reshape(gram_shape))
-    return r_sum, gram_sum.reshape(256, 256)
+    )(r_part, gram_part.reshape(gram_shape), sketch, coef_t)
 
 
 def per_device(tokens, cotangent, gate_logit, routes, w_up, w_down, basis, sketch):
@@ -408,20 +493,17 @@
     r_part, coef_t, gram_part = gather_compute(
         arrived[:width_local], arrived[width_local:], basis, w_up[0], w_down[0], deep
     )
-    r_sum, gram_total = reduce_all(r_part, gram_part, deep)
-    rows = jnp.pad(r_sum.T, ((0, 0), (0, 128 - width_local)))
-    returned = exchange(rows.reshape(experts, capacity, 128), experts, 3)
+    hidden_total = w_up.shape[1] * lax.axis_size("dp")
+    returned, merged, solved_t = reduce_all(
+        r_part, gram_part, sketch[0], coef_t, deep, experts, hidden_total
+    )
     token_grad = lax.dot_general(
         table_b,
         returned.reshape(slot_count, 128)[:, :width_local],
         (((0,), (0,)), ((), ())),
         preferred_element_type=f32,
     ).astype(bf16)
-    total_hidden = w_up.shape[1] * lax.axis_size("dp")
-    merged = decay_rate * sketch[0] + gram_total / total_hidden
-    factor = jnp.linalg.cholesky(merged + damping * jnp.eye(merged.shape[0], dtype=f32))
-    solved = damping * jax.scipy.linalg.cho_solve((factor, True), coef_t.T)
-    return (token_grad, merged[None], solved.T[None])
+    return (token_grad, merged[None], solved_t[None])
 
 
 def solution(mesh):

time: 181 us -> 130 us (0.72); the launches traced: 178 us -> 129 us
  other arithmetic: 57.2 us -> 2.5 us
  Pallas kernels: 102 us -> 117 us
  local copies, waits for them, and re-layouts: 11.1 us -> 6.71 us
  matrix products: 5.18 us -> 2.34 us
    another operation x9 -> x0, other arithmetic: 53.9 us -> none  [the longest x6 33.9 us: per_device(): jnp.linalg.cholesky(merged + damping * jnp.eye(merged.shape[0], dtype=f32))]
    pallas_call x1, Pallas kernels: 28.5 us -> 50.9 us  [reduce_all(): pl.pallas_call(functools.partial(reduce_kernel, deep, experts, hidden_tot...]
    pallas_call x2 -> x1, Pallas kernels: 20.1 us -> 10.7 us  [exchange(): pl.pallas_call(functools.partial(exchange_kernel, n), out_shape=jax.Shape...]
    another operation x9 -> x0, local copies, waits for them, and re-layouts: 4.05 us -> none
    another operation x8 -> x0, matrix products: 2.01 us -> none  [the longest x6 1.54 us: per_device(): solved = damping * jax.scipy.linalg.cho_solve((factor, True), coef_t.T)]
    pallas_call x1, Pallas kernels: 53.7 us -> 55.6 us  [gather_compute(): pl.pallas_call(functools.partial(gather_kernel, deep), out_shape=(jax.Sha...]
    unnamed x11 -> x10, local copies, waits for them, and re-layouts: 4.84 us -> 4.86 us
where the time goes in v2:
time: 130 us; the launch traced here: 129 us
  Pallas kernels  117 us (90%)
  local copies, waits for them, and re-layouts  6.71 us (5%)
  other arithmetic  2.5 us (2%)
  matrix products  2.34 us (2%)
    pallas_call x1, Pallas kernels, gather_compute(): pl.pallas_call(functools.partial(gather_kernel, deep), out_shape=(jax.Sha...  55.6 us
    pallas_call x1, Pallas kernels, reduce_all(): pl.pallas_call(functools.partial(reduce_kernel, deep, experts, hidden_tot...  50.9 us
    pallas_call x1, Pallas kernels, exchange(): pl.pallas_call(functools.partial(exchange_kernel, n), out_shape=jax.Shape...  10.7 us
    unnamed x10, local copies, waits for them, and re-layouts  4.86 us

profile of v2, /device:TPU:1, one launch (start us, length us, event | category | flops | bytes accessed | tf_op | source)
XLA Modules:
  0.0 129.5 jit_solution(14420104344435928527)
XLA Ops:
  0.7 0.7 subtract_bitcast_fusion
  1.3 0.7 select_reduce_fusion.1
  2.0 0.7 convert_reduce_fusion.1
  2.7 0.1 copy.19
  2.8 0.1 copy.17
  2.9 0.1 copy.20
  3.0 0.1 reduce_window_sum.11
  3.1 0.3 convert_reduce_fusion
  3.4 1.6 %fusion = bf16[256,128]{1,0:T(8,128)(2,1)} fusion(f32[256]{0:T(256)S(1)} %get-tuple-element.16, pred[128]{0:T(512)(128)(4,1)S(1)} %iota_compare_fusion.2, bf16[64,64]{1,0:T(8,128)(2,1)} %param.9, bf16[64,64]{1,0:T(8,128)(2,1)} %param.8, bf16[256,64]{0,1:T(8,128)(2,1)S(1)} %get-tuple-element.15), kind=kOutput, calls=%fused_computation.1 | convolution fusion | flops 4325376 | bytes 115840 | tf_op jit(solution)/shard_map/dot_general | solution.py:489
  5.0 10.7 %shard_map.103 = bf16[8,32,128]{2,1,0:T(8,128)(2,1)} custom-call(bf16[8,32,128]{2,1,0:T(8,128)(2,1)} %bitcast.24), custom_call_target="tpu_custom_call" | custom-call | tf_op jit(solution)/shard_map/pallas_call | solution.py:58
  15.7 0.9 copy.21
  16.7 0.6 fusion.9
  17.3 0.0 copy-start.1
  17.3 55.6 %shard_map.104 = (bf16[8,4,2,64,256]{4,3,2,1,0:T(8,128)(2,1)}, f32[224,256]{1,0:T(8,128)}, f32[256,256]{1,0:T(8,128)}) custom-call(bf16[64,256]{1,0:T(8,128)(2,1)} %get-tuple-element.20.x_in, bf16[64,256]{1,0:T(8,128)(2,1)} %get-tuple-element.19.dy_in, bf16[64,256]{1,0:T(8,128)(2,1)} %basis_in.1, bf16[224,4096]{1,0:T(8,128)(2,1)} %bitcast.20, ...), custom_call_target="tpu_custom_call" | custom-call | tf_op jit(solution)/shard_map/pallas_call | solution.py:230
  72.9 0.0 copy-done.1
  73.0 0.0 copy-start
  73.0 1.6 %copy-done = bf16[8,4,2,64,256]{4,3,2,1,0:T(8,128)(2,1)S(1)} copy-done((bf16[8,4,2,64,256]{4,3,2,1,0:T(8,128)(2,1)S(1)}, bf16[8,4,2,64,256]{4,3,2,1,0:T(8,128)(2,1)}, u32[]{:S(2)}) %copy-start) | copy-done | bytes 2097176
  74.6 0.0 copy-start.2
  74.6 0.9 copy-done.2
  75.5 0.0 copy-start.3
  75.5 0.9 copy-done.3
  76.4 50.9 %shard_map.105 = (bf16[8,32,128]{2,1,0:T(8,128)(2,1)S(1)}, f32[256,256]{1,0:T(8,128)S(1)}, f32[224,256]{1,0:T(8,128)S(1)}) custom-call(bf16[8,4,2,64,256]{4,3,2,1,0:T(8,128)(2,1)S(1)} %copy-done, f32[2,4,32,256]{3,2,1,0:T(8,128)S(1)} %bitcast.17, f32[256,256]{1,0:T(8,128)S(1)} %bitcast.16, f32[224,256]{1,0:T(8,128)S(1)} %copy-done.3), custom_call_target="tpu_custom_call" | custom-call | tf_op jit(solution)/shard_map/pallas_call | solution.py:430
  127.3 0.7 convolution_convert_fusion
  128.1 0.7 copy.24
  128.8 0.7 copy.25
  (5 shorter events, 0.0 us)
Async XLA Ops:
  17.3 55.6 %copy-start.1 = (f32[1,256,256]{2,1,0:T(8,128)S(1)}, f32[1,256,256]{2,1,0:T(8,128)}, u32[]{:S(2)}) copy-start(f32[1,256,256]{2,1,0:T(8,128)} %param.15) | copy-start | bytes 786436
  73.0 1.6 %copy-start = (bf16[8,4,2,64,256]{4,3,2,1,0:T(8,128)(2,1)S(1)}, bf16[8,4,2,64,256]{4,3,2,1,0:T(8,128)(2,1)}, u32[]{:S(2)}) copy-start(bf16[8,4,2,64,256]{4,3,2,1,0:T(8,128)(2,1)} %get-tuple-element.9.r_in) | copy-start | bytes 6291460
  74.6 0.9 copy-start.2
  75.5 0.9 copy-start.3

commit v3 on v2

--- a/solution.py
+++ b/solution.py
@@ -16,7 +16,7 @@
 bf16 = jnp.bfloat16
 f32 = jnp.float32
 VMEM = pl.BlockSpec(memory_space=pltpu.VMEM)
-ANY = pl.BlockSpec(memory_space=pl.ANY)
+HBM = pl.BlockSpec(memory_space=pltpu.HBM)
 
 
 def greet(axis, peers):
@@ -65,7 +65,9 @@
             pltpu.SemaphoreType.DMA((n,)),
             pltpu.SemaphoreType.DMA,
         ],
-        compiler_params=pltpu.CompilerParams(collective_id=number, has_side_effects=True),
+        compiler_params=pltpu.CompilerParams(
+            collective_id=number, has_side_effects=True, vmem_limit_bytes=4 << 20
+        ),
     )(value)
 
 
@@ -83,6 +85,7 @@
 def gather_kernel(
     deep, x_in, dy_in, basis_in, up_hbm, down_hbm, r_out, c_out, gram_out,
     xs, dys, bases, up, down, hid, back, proj, sent, got, ring_send, ring_recv, share_send, share_recv,
+    early_send, early_recv,
 ):
     z, x, core = place(deep)
     other = 1 - core
@@ -154,15 +157,37 @@
 
     def stages(t):
         first, second = orders[t]
-        for step in range(1, sizes[first] // 2 + 1):
+        n = sizes[second]
+        count = sizes[first]
+        early = []
+
+        def pass_on(at, source=None):
+            piece = block(t, first, at)
+            number = len(early) // 2
+            for way, sign in enumerate((1, -1)):
+                early.append(
+                    remote(
+                        piece if source is None else source, piece,
+                        early_send.at[t, way, number], early_recv.at[t, way, number],
+                        "dp", near(second, sign),
+                    )
+                )
+
+        for step in range(1, count // 2 + 1):
             copies = ring_step(t, 0, first, step, block)
+            if step == 1 and n > 2:
+                pass_on(spot[first], starts[t])
             yield
             for copy in copies:
                 copy.wait_recv()
+            if n > 2:
+                pass_on(lax.rem(spot[first] - step + count, count))
+                if step < count // 2:
+                    pass_on(lax.rem(spot[first] + step, count))
         own[t].wait()
         at = spot[second]
-        n = sizes[second]
-        copies = ring_step(t, 1, second, 1, slab)
+        sends.extend(early)
+        copies = early if n > 2 else ring_step(t, 1, second, 1, slab)
         share(t, second, at)
         yield
         for step in range(1, n // 2):
@@ -234,7 +259,7 @@
             jax.ShapeDtypeStruct((units, 256), f32),
             jax.ShapeDtypeStruct((256, 256), f32),
         ),
-        in_specs=[VMEM, VMEM, VMEM, ANY, ANY],
+        in_specs=[VMEM, VMEM, VMEM, HBM, HBM],
         out_specs=(VMEM, VMEM, VMEM),
         scratch_shapes=[
             pltpu.VMEM(blocks, bf16),
@@ -251,14 +276,16 @@
             pltpu.SemaphoreType.DMA((3, 2, 2, steps // 2)),
             pltpu.SemaphoreType.DMA((3, steps)),
             pltpu.SemaphoreType.DMA((3, steps)),
+            pltpu.SemaphoreType.DMA((3, 2, steps)),
+            pltpu.SemaphoreType.DMA((3, 2, steps)),
         ],
         compiler_params=pltpu.CompilerParams(
-            collective_id=1, has_side_effects=True, vmem_limit_bytes=60 << 20
+            collective_id=1, has_side_effects=True, vmem_limit_bytes=52 << 20
         ),
     )(x_t, dy_t, basis, up, down)
 
 
-def invert(matrix):
+def eliminate(matrix, rounds):
     n, group = 128, 16
     lane = lax.broadcasted_iota(jnp.int32, (1, n), 1)
     row = lax.broadcasted_iota(jnp.int32, (group, n), 0)
@@ -289,7 +316,7 @@
         turned = pltpu.roll(jnp.concatenate([rest, top], axis=0), n - group, 1)
         return turned[:group], turned[group:]
 
-    top, rest = lax.fori_loop(0, n // group, pivots, (matrix[:group], matrix[group:]))
+    top, rest = lax.fori_loop(0, rounds, pivots, (matrix[:group], matrix[group:]))
     return jnp.concatenate([top, rest], axis=0)
 
 
@@ -377,7 +404,7 @@
         == lax.broadcasted_iota(jnp.int32, (half, half), 1)
     ).astype(f32) * damping
     corner = merged[:half, half:]
-    upper = invert(merged[:half, :half] + eye)
+    upper = eliminate(merged[:half, :half] + eye, 8)
     ratio = exact(upper, corner)
     lower = merged[half:, half:] + eye - exact(merged[half:, :half], ratio)
 
@@ -397,6 +424,7 @@
     left, right = coef_in[:, :half], coef_in[:, half:]
     right = right - exact(left, ratio)
     left = exact(left, upper)
+    lower = eliminate(lower, 4)
     for copy in r_z:
         copy.wait_recv()
     part = r1[z].astype(f32)
@@ -411,7 +439,7 @@
     mine = pltpu.make_async_copy(ready.at[me_y], back_out.at[me_y], y_own)
     mine.start()
 
-    right = exact(right, invert(lower))
+    right = exact(right, eliminate(lower, 4))
     solved_out[:, half:] = right * damping
     left = left - exact(right, ratio, (((1,), (1,)), ((), ())))
     solved_out[:, :half] = left * damping

time: 130 us -> 118 us (0.908)
  Pallas kernels: 117 us -> 108 us
  local copies, waits for them, and re-layouts: 6.71 us -> 4.12 us
    pallas_call x1, Pallas kernels: 55.6 us -> 49.5 us  [gather_compute(): pl.pallas_call(functools.partial(gather_kernel, deep), out_shape=(jax.Sha...]
    pallas_call x1, Pallas kernels: 10.7 us -> 9.3 us  [exchange(): pl.pallas_call(functools.partial(exchange_kernel, n), out_shape=jax.Shape...]
    unnamed x10 -> x8, local copies, waits for them, and re-layouts: 4.86 us -> 3.73 us
where the time goes in v3:
time: 118 us
  Pallas kernels  108 us (92%)
  local copies, waits for them, and re-layouts  4.12 us (3%)
  other arithmetic  2.5 us (2%)
  matrix products  1.7 us (1%)
    pallas_call x1, Pallas kernels, reduce_all(): pl.pallas_call(functools.partial(reduce_kernel, deep, experts, hidden_tot...  49.7 us
    pallas_call x1, Pallas kernels, gather_compute(): pl.pallas_call(functools.partial(gather_kernel, deep), out_shape=(jax.Sha...  49.5 us
    pallas_call x1, Pallas kernels, exchange(): pl.pallas_call(functools.partial(exchange_kernel, n), out_shape=jax.Shape...  9.3 us
    unnamed x8, local copies, waits for them, and re-layouts  3.73 us

profile of v3, /device:TPU:1, one launch (start us, length us, event | category | flops | bytes accessed | tf_op | source)
XLA Modules:
  0.0 117.5 jit_solution(7186876723614377859)
XLA Ops:
  0.7 0.7 subtract_bitcast_fusion
  1.3 0.7 select_reduce_fusion.1
  2.0 0.7 convert_reduce_fusion.1
  2.7 0.1 copy.19
  2.8 0.1 copy.17
  2.9 0.1 copy.20
  3.0 0.1 reduce_window_sum.11
  3.1 0.3 convert_reduce_fusion
  3.4 1.0 fusion
  4.4 9.3 %shard_map.103 = bf16[8,32,128]{2,1,0:T(8,128)(2,1)S(1)} custom-call(bf16[8,32,128]{2,1,0:T(8,128)(2,1)S(1)} %bitcast.21), custom_call_target="tpu_custom_call" | custom-call | tf_op jit(solution)/shard_map/pallas_call | solution.py:58
  13.7 0.1 copy.21
  13.8 0.0 copy-start.2
  13.8 0.7 copy-done.2
  14.6 0.0 copy-start.1
  14.6 49.5 %shard_map.104 = (bf16[8,4,2,64,256]{4,3,2,1,0:T(8,128)(2,1)}, f32[224,256]{1,0:T(8,128)S(1)}, f32[256,256]{1,0:T(8,128)S(1)}) custom-call(bf16[64,256]{1,0:T(8,128)(2,1)S(1)} %get-tuple-element.20.x_in, bf16[64,256]{1,0:T(8,128)(2,1)S(1)} %get-tuple-element.19.dy_in, bf16[64,256]{1,0:T(8,128)(2,1)S(1)} %copy-done.2, bf16[224,4096]{1,0:T(8,128)(2,1)} %bitcast.22, ...), custom_call_target="tpu_custom_call" | custom-call | tf_op jit(solution)/shard_map/pallas_call | solution.py:255
  64.1 0.0 copy-done.1
  64.1 0.0 copy-start
  64.1 1.6 %copy-done = bf16[8,4,2,64,256]{4,3,2,1,0:T(8,128)(2,1)S(1)} copy-done((bf16[8,4,2,64,256]{4,3,2,1,0:T(8,128)(2,1)S(1)}, bf16[8,4,2,64,256]{4,3,2,1,0:T(8,128)(2,1)}, u32[]{:S(2)}) %copy-start) | copy-done | bytes 2097176
  65.7 49.7 %shard_map.105 = (bf16[8,32,128]{2,1,0:T(8,128)(2,1)S(1)}, f32[256,256]{1,0:T(8,128)S(1)}, f32[224,256]{1,0:T(8,128)S(1)}) custom-call(bf16[8,4,2,64,256]{4,3,2,1,0:T(8,128)(2,1)S(1)} %copy-done, f32[2,4,32,256]{3,2,1,0:T(8,128)S(1)} %bitcast.18, f32[256,256]{1,0:T(8,128)S(1)} %bitcast.17, f32[224,256]{1,0:T(8,128)S(1)} %get-tuple-element.11.coef_in), custom_call_target="tpu_custom_call" | custom-call | tf_op jit(solution)/shard_map/pallas_call | solution.py:458
  115.4 0.7 convolution_convert_fusion
  116.1 0.7 copy.24
  116.8 0.7 copy.25
  (6 shorter events, 0.0 us)
Async XLA Ops:
  13.8 0.8 copy-start.2
  14.6 49.5 %copy-start.1 = (f32[1,256,256]{2,1,0:T(8,128)S(1)}, f32[1,256,256]{2,1,0:T(8,128)}, u32[]{:S(2)}) copy-start(f32[1,256,256]{2,1,0:T(8,128)} %param.15) | copy-start | bytes 786436
  64.1 1.6 %copy-start = (bf16[8,4,2,64,256]{4,3,2,1,0:T(8,128)(2,1)S(1)}, bf16[8,4,2,64,256]{4,3,2,1,0:T(8,128)(2,1)}, u32[]{:S(2)}) copy-start(bf16[8,4,2,64,256]{4,3,2,1,0:T(8,128)(2,1)} %get-tuple-element.9.r_in) | copy-start | bytes 6291460

commit v4 on v3

--- a/solution.py
+++ b/solution.py
@@ -341,9 +341,10 @@
     barrier = pltpu.get_barrier_semaphore()
     for peer in y_at:
         pl.semaphore_signal(barrier, inc=1, device_id={"expert": peer}, device_id_type=MESH)
-    for peer in [partner] + x_peers + z_peers:
+    cross_peers = [index_of(z, at, other) for at in x_at]
+    for peer in [partner] + x_peers + cross_peers + z_peers:
         pl.semaphore_signal(barrier, inc=1, device_id={"dp": peer}, device_id_type=MESH)
-    pl.semaphore_wait(barrier, 1 + len(x_peers) + len(z_peers) + len(y_at))
+    pl.semaphore_wait(barrier, 1 + 2 * len(x_peers) + len(z_peers) + len(y_at))
 
     def to_core(number, src, dst):
         return remote(src, dst, core_send.at[number], core_recv.at[number], "dp", partner)
@@ -366,14 +367,6 @@
     gram_core.wait_recv()
     gsum[...] = gram_in[core] + g0[...]
     gram_x = along_x(0, [(gsum.at[at], gx.at[x]) for at in x_at])
-
-    r_core.wait_recv()
-
-    def add_core(at, carry):
-        rsum[at] = (r_in[at, :, core].astype(f32) + r0[at].astype(f32)).astype(bf16)
-        return carry
-
-    lax.fori_loop(0, deep, add_core, 0)
 
     for copy in gram_x:
         copy.wait_recv()
@@ -382,7 +375,15 @@
         total = total + gx[at]
     gz[z] = total
     gram_z = along_z(0, [(gz.at[z], gz.at[z]) for _ in z_at])
-    r_x = along_x(1, [(rsum.at[:, at], rx.at[x]) for at in x_at])
+
+    r_core.wait_recv()
+
+    def add_core(at, carry):
+        rsum[at] = (r_in[at, :, core].astype(f32) + r0[at].astype(f32)).astype(bf16)
+        return carry
+
+    lax.fori_loop(0, deep, add_core, 0)
+
 
     for copy in gram_z:
         copy.wait_recv()
@@ -391,10 +392,16 @@
         total = total + gz[at]
     gram_out[core, x] = total
     gram_back = along_x(2, [(gram_out.at[core, x], gram_out.at[core, x]) for _ in x_at])
+    piece = gram_out.at[core, x]
+    gram_back += [
+        remote(piece, piece, x_send.at[3, k], x_recv.at[3, k], "dp", peer)
+        for k, peer in enumerate(cross_peers)
+    ]
+    gram_last = to_core(2, piece, piece)
+    r_x = along_x(1, [(rsum.at[:, at], rx.at[x]) for at in x_at])
+    gram_last.wait_recv()
     for copy in gram_back:
         copy.wait_recv()
-    gram_last = to_core(2, gram_out.at[core], gram_out.at[core])
-    gram_last.wait_recv()
 
     merged = decay_rate * sketch_in[...] + gram_out[...].reshape(256, 256) / hidden_total
     merged_out[...] = merged
@@ -478,8 +485,8 @@
             pltpu.VMEM(send_shape, bf16),
             pltpu.SemaphoreType.DMA((3,)),
             pltpu.SemaphoreType.DMA((3,)),
-            pltpu.SemaphoreType.DMA((3, WIDE)),
-            pltpu.SemaphoreType.DMA((3, WIDE)),
+            pltpu.SemaphoreType.DMA((4, WIDE)),
+            pltpu.SemaphoreType.DMA((4, WIDE)),
             pltpu.SemaphoreType.DMA((2, deep)),
             pltpu.SemaphoreType.DMA((2, deep)),
             pltpu.SemaphoreType.DMA((experts,)),

time: 118 us -> 116 us (0.983)
  Pallas kernels: 108 us -> 106 us
    pallas_call x1, Pallas kernels: 49.7 us -> 46.9 us  [reduce_all(): pl.pallas_call(functools.partial(reduce_kernel, deep, experts, hidden_tot...]
where the time goes in v4:
time: 116 us; the launch traced here: 115 us
  Pallas kernels  106 us (91%)
  local copies, waits for them, and re-layouts  4.12 us (4%)
  other arithmetic  2.5 us (2%)
  matrix products  1.7 us (1%)
    pallas_call x1, Pallas kernels, gather_compute(): pl.pallas_call(functools.partial(gather_kernel, deep), out_shape=(jax.Sha...  49.5 us
    pallas_call x1, Pallas kernels, reduce_all(): pl.pallas_call(functools.partial(reduce_kernel, deep, experts, hidden_tot...  46.9 us
    pallas_call x1, Pallas kernels, exchange(): pl.pallas_call(functools.partial(exchange_kernel, n), out_shape=jax.Shape...  9.3 us
    unnamed x8, local copies, waits for them, and re-layouts  3.73 us

profile of v4, /device:TPU:1, one launch (start us, length us, event | category | flops | bytes accessed | tf_op | source)
XLA Modules:
  0.0 114.8 jit_solution(12292023092830328940)
XLA Ops:
  0.7 0.7 subtract_bitcast_fusion
  1.3 0.7 select_reduce_fusion.1
  2.0 0.7 convert_reduce_fusion.1
  2.7 0.1 copy.19
  2.8 0.1 copy.17
  2.9 0.1 copy.20
  3.0 0.1 reduce_window_sum.11
  3.1 0.3 convert_reduce_fusion
  3.4 1.0 fusion
  4.4 9.3 %shard_map.103 = bf16[8,32,128]{2,1,0:T(8,128)(2,1)S(1)} custom-call(bf16[8,32,128]{2,1,0:T(8,128)(2,1)S(1)} %bitcast.21), custom_call_target="tpu_custom_call" | custom-call | tf_op jit(solution)/shard_map/pallas_call | solution.py:58
  13.7 0.1 copy.21
  13.8 0.0 copy-start.2
  13.8 0.7 copy-done.2
  14.6 0.0 copy-start.1
  14.6 49.5 %shard_map.104 = (bf16[8,4,2,64,256]{4,3,2,1,0:T(8,128)(2,1)}, f32[224,256]{1,0:T(8,128)S(1)}, f32[256,256]{1,0:T(8,128)S(1)}) custom-call(bf16[64,256]{1,0:T(8,128)(2,1)S(1)} %get-tuple-element.20.x_in, bf16[64,256]{1,0:T(8,128)(2,1)S(1)} %get-tuple-element.19.dy_in, bf16[64,256]{1,0:T(8,128)(2,1)S(1)} %copy-done.2, bf16[224,4096]{1,0:T(8,128)(2,1)} %bitcast.22, ...), custom_call_target="tpu_custom_call" | custom-call | tf_op jit(solution)/shard_map/pallas_call | solution.py:255
  64.1 0.0 copy-done.1
  64.1 0.0 copy-start
  64.1 1.6 %copy-done = bf16[8,4,2,64,256]{4,3,2,1,0:T(8,128)(2,1)S(1)} copy-done((bf16[8,4,2,64,256]{4,3,2,1,0:T(8,128)(2,1)S(1)}, bf16[8,4,2,64,256]{4,3,2,1,0:T(8,128)(2,1)}, u32[]{:S(2)}) %copy-start) | copy-done | bytes 2097176
  65.7 46.9 %shard_map.105 = (bf16[8,32,128]{2,1,0:T(8,128)(2,1)S(1)}, f32[256,256]{1,0:T(8,128)S(1)}, f32[224,256]{1,0:T(8,128)S(1)}) custom-call(bf16[8,4,2,64,256]{4,3,2,1,0:T(8,128)(2,1)S(1)} %copy-done, f32[2,4,32,256]{3,2,1,0:T(8,128)S(1)} %bitcast.18, f32[256,256]{1,0:T(8,128)S(1)} %bitcast.17, f32[224,256]{1,0:T(8,128)S(1)} %get-tuple-element.11.coef_in), custom_call_target="tpu_custom_call" | custom-call | tf_op jit(solution)/shard_map/pallas_call | solution.py:465
  112.7 0.7 convolution_convert_fusion
  113.4 0.7 copy.24
  114.1 0.7 copy.25
  (6 shorter events, 0.0 us)
Async XLA Ops:
  13.8 0.8 copy-start.2
  14.6 49.5 %copy-start.1 = (f32[1,256,256]{2,1,0:T(8,128)S(1)}, f32[1,256,256]{2,1,0:T(8,128)}, u32[]{:S(2)}) copy-start(f32[1,256,256]{2,1,0:T(8,128)} %param.15) | copy-start | bytes 786436
  64.1 1.6 %copy-start = (bf16[8,4,2,64,256]{4,3,2,1,0:T(8,128)(2,1)S(1)}, bf16[8,4,2,64,256]{4,3,2,1,0:T(8,128)(2,1)}, u32[]{:S(2)}) copy-start(bf16[8,4,2,64,256]{4,3,2,1,0:T(8,128)(2,1)} %get-tuple-element.9.r_in) | copy-start | bytes 6291460
